TPU v7x, 256 devices: a whole 4x4x8 slice. The times are simulated.
256 devices in a mesh: smp: 32 (over x_lo, z, core), par: 8 (over x_hi, y).
Axes of the slice: x: 4 (x_hi: 2, x_lo: 2; x = x_hi * 2 + x_lo), y: 4, z: 8, core: 2. Of those that a mesh axis runs over, the one named last changes fastest.
Arguments:
- log_derivs: float32 [8192, 8192], P('smp', 'par'), may hold values from -40 to 40, as said below
- coefficients: float32 [8192], P('smp'), may hold values from -6 to 6
Outputs:
- gram: float32 [8192, 8192], P('smp', 'par')
- update: float32 [8192], P(('par', 'smp'))
Inputs may be any that keep to these rules, and one draw needn't show every extreme that they name: `log_derivs`: finite real values.
All inputs are finite; a program needn't handle non-finite values.
Results may differ from a plain program's by a relative error of at most 0.00014.
Values sent between devices are 32-bit elements; how exact they have to be, the bound alone decides.
A program may use at most 128 MiB of HBM per device.

v0:
```python
import jax
import jax.numpy as jnp
from jax import lax
from jax.sharding import PartitionSpec as P


def row_products(left_rows, right_rows):
    return lax.dot_general(
        left_rows,
        right_rows,
        (((1,), (1,)), ((), ())),
        precision=lax.Precision.HIGHEST,
        preferred_element_type=jnp.float32,
    )


def local(log_derivs, coefficients):
    samples = log_derivs.shape[0] * lax.axis_size("smp")
    column_total = lax.psum(jnp.sum(log_derivs, axis=0), "smp")
    centred = (log_derivs - column_total[None, :] / samples) / jnp.sqrt(jnp.float32(samples))
    partial_gram = row_products(centred, lax.all_gather(centred, "smp", axis=0, tiled=True))
    gram = lax.psum_scatter(partial_gram, "par", scatter_dimension=1, tiled=True)
    update_term = lax.dot_general(
        coefficients,
        centred,
        (((0,), (0,)), ((), ())),
        precision=lax.Precision.HIGHEST,
        preferred_element_type=jnp.float32,
    )
    update = lax.psum_scatter(update_term, "smp", scatter_dimension=0, tiled=True)
    return (gram, update)


def solution(mesh):
    placed = (P("smp", "par"), P("smp"))
    return jax.shard_map(
        local,
        mesh=mesh,
        in_specs=placed,
        out_specs=(P("smp", "par"), P(("par", "smp"))),
        check_vma=False,
    )
```

profile of v0, /device:TPU:1, one launch (start us, length us, event | category | flops | bytes accessed | tf_op | source)
XLA Modules:
  0.0 410.7 jit_solution(7156183414748305137)
XLA Ops:
  7.2 0.0 copy-start
  7.2 0.0 all-gather.2.cloned.1.call-start
  7.2 1.3 reduce_sum.9
  8.5 56.9 %psum.7 = f32[1024]{0:T(1024)S(1)} all-reduce(f32[1024]{0:T(1024)S(1)} %reduce_sum.9), channel_id=1, replica_groups=mesh['smp'=32,'par'=8] {'smp'}, use_global_device_ids=true, to_apply=%region_1.0 | all-reduce | flops 1024 | bytes 8192 | tf_op jit(solution)/shard_map/psum | solution.py:19
  65.4 2.4 subtract_multiply_fusion
  67.8 0.0 all-gather.2.cloned.1.call-update
  67.8 0.0 copy-start.2
  67.8 0.0 copy-start.1
  67.9 0.0 reduce-scatter.2.cloned.1.call-start
  67.9 183.8 %all-gather.2.cloned.1.call-done = f32[8192,1024]{1,0:T(8,128)} async-done(((f32[256,1024]{1,0:T(8,128)}), f32[8192,1024]{1,0:T(8,128)}) %all-gather.2.cloned.1.call-update) | async-done | bytes 33554448 | tf_op jit(solution)/shard_map/all_gather | solution.py:21
  251.7 33.2 %fusion = f32[256,8192]{1,0:T(8,128)} fusion(f32[256,1024]{1,0:T(8,128)} %subtract_multiply_fusion, f32[8192,1024]{1,0:T(8,128)} %all-gather.2.cloned.1.call-done), kind=kOutput, calls=%fused_computation.2 | convolution fusion | flops 25769803776 | bytes 42991616 | tf_op jit(solution)/shard_map/dot_general | solution.py:8
  284.9 0.0 reduce-scatter.2.cloned.1.call-update
  285.0 0.0 copy-done.2
  285.0 0.6 dynamic-slice
  286.2 0.0 copy-done
  286.2 0.0 copy-done.1
  286.2 0.6 fusion.1
  286.9 53.7 %all-reduce = f32[1024]{0:T(1024)S(1)} all-reduce(f32[1024]{0:T(1024)S(1)} %bitcast.8), channel_id=3, replica_groups=mesh['smp'=32,'par'=8] {'smp'}, use_global_device_ids=true, to_apply=%region_3.0.clone | all-reduce | flops 1024 | bytes 8192
  340.6 0.6 dynamic-slice.1
  341.2 62.6 %reduce-scatter.2.cloned.1.call-done = f32[256,1024]{1,0:T(8,128)} async-done(((f32[256,8192]{1,0:T(8,128)}), f32[256,1024]{1,0:T(8,128)}) %reduce-scatter.2.cloned.1.call-update) | async-done | bytes 1048592 | tf_op jit(solution)/shard_map/reduce_scatter | solution.py:22
  (1 shorter events, 0.0 us)
Async XLA Ops:
  7.2 279.1 %copy-start = (f32[256]{0:T(256)S(1)}, f32[256]{0:T(256)}, u32[]{:S(2)}) copy-start(f32[256]{0:T(256)} %param.3) | copy-start | bytes 3076
  7.2 244.5 %all-gather.2.cloned.1.call-start = ((), (), s32[]{:S(2)}) async-start(), calls=%async_computation.1 | async-start | bytes 34603008 | tf_op jit(solution)/shard_map/all_gather | solution.py:21
  67.8 217.1 %copy-start.2 = (u32[256]{0:T(256)S(1)}, u32[256]{0:T(256)}, u32[]{:S(2)}) copy-start(u32[256]{0:T(256)} %constant.10) | copy-start | bytes 3076
  67.8 218.4 %copy-start.1 = (f32[256,1024]{1,0:T(8,128)S(1)}, f32[256,1024]{1,0:T(8,128)}, u32[]{:S(2)}) copy-start(f32[256,1024]{1,0:T(8,128)} %subtract_multiply_fusion) | copy-start | bytes 3145732
  67.9 336.0 %reduce-scatter.2.cloned.1.call-start = ((), (), s32[]{:S(2)}) async-start(), calls=%async_computation.2 | async-start | bytes 9437184 | tf_op jit(solution)/shard_map/reduce_scatter | solution.py:22
Sparse Core Ops, SparseCore 0:
  67.9 183.7 all-gather.1
  285.1 118.6 reduce-scatter.1
where the time goes:
time: 411 us
  waiting for transfers between devices  246 us (60%)
  blocking collectives  111 us (27%)
  matrix products  33.9 us (8%)
  between operations  14.7 us (4%)
    all_gather x1, waiting for transfers between devices, local(): lax.all_gather(centred, 'smp', axis=0, tiled=True)  184 us
    reduce_scatter x1, waiting for transfers between devices, local(): lax.psum_scatter(partial_gram, 'par', scatter_dimension=1, tiled=True)  62.6 us
    psum x1, blocking collectives, local(): column_total = lax.psum(jnp.sum(log_derivs, axis=0), 'smp')  56.9 us
    unnamed x1, blocking collectives  53.7 us
    dot_general x1, matrix products, row_products(): lax.dot_general(left_rows, right_rows, (((1,), (1,)), ((), ())), precisio...  33.2 us
  transfers between devices with their start and end apart: 2, of which 2 were waited for; matrix products, arithmetic and copies ran while one was open for 0% of the time, Pallas kernels for 0%

commit v1 on v0

--- a/solution.py
+++ b/solution.py
@@ -16,7 +16,7 @@
 
 def local(log_derivs, coefficients):
     samples = log_derivs.shape[0] * lax.axis_size("smp")
-    column_total = lax.psum(jnp.sum(log_derivs, axis=0), "smp")
+    column_total = jnp.sum(lax.all_gather(jnp.sum(log_derivs, axis=0), "smp"), axis=0)
     centred = (log_derivs - column_total[None, :] / samples) / jnp.sqrt(jnp.float32(samples))
     partial_gram = row_products(centred, lax.all_gather(centred, "smp", axis=0, tiled=True))
     gram = lax.psum_scatter(partial_gram, "par", scatter_dimension=1, tiled=True)

time: 411 us -> 389 us (0.946)
  blocking collectives: 111 us -> 92.5 us
    psum x1 -> x0, blocking collectives: 56.9 us -> none  [local(): column_total = lax.psum(jnp.sum(log_derivs, axis=0), 'smp')]
    all_gather x0 -> x1, blocking collectives: none -> 38.8 us  [local(): lax.all_gather(jnp.sum(log_derivs, axis=0), 'smp')]
where the time goes in v1:
time: 389 us
  waiting for transfers between devices  243 us (62%)
  blocking collectives  92.5 us (24%)
  matrix products  33.9 us (9%)
  between operations  14.8 us (4%)
    all_gather x1, waiting for transfers between devices, local(): lax.all_gather(centred, 'smp', axis=0, tiled=True)  180 us
    reduce_scatter x1, waiting for transfers between devices, local(): lax.psum_scatter(partial_gram, 'par', scatter_dimension=1, tiled=True)  62.4 us
    unnamed x1, blocking collectives  53.7 us
    all_gather x1, blocking collectives, local(): lax.all_gather(jnp.sum(log_derivs, axis=0), 'smp')  38.8 us
    dot_general x1, matrix products, row_products(): lax.dot_general(left_rows, right_rows, (((1,), (1,)), ((), ())), precisio...  33.2 us
  transfers between devices with their start and end apart: 2, of which 2 were waited for; matrix products, arithmetic and copies ran while one was open for 0% of the time, Pallas kernels for 0%

profile of v1, /device:TPU:1, one launch (start us, length us, event | category | flops | bytes accessed | tf_op | source)
XLA Modules:
  0.0 388.8 jit_solution(12788124747997990614)
XLA Ops:
  7.2 0.0 copy-start
  7.2 0.0 all-gather.3.cloned.1.call-start
  7.2 1.3 reduce_sum.18
  8.5 38.8 %all-gather = f32[32768]{0:T(1024)S(1)} all-gather(f32[1024]{0:T(1024)S(1)} %reduce_sum.18), channel_id=2, replica_groups=mesh['smp'=32,'par'=8] {'smp'}, dimensions={0}, use_global_device_ids=true | all-gather | bytes 135168 | tf_op jit(solution)/shard_map/all_gather | solution.py:19
  47.4 2.4 subtract_multiply_fusion
  49.8 0.0 all-gather.3.cloned.1.call-update
  49.8 0.0 copy-start.2
  49.8 0.0 copy-start.1
  49.8 0.0 reduce-scatter.2.cloned.1.call-start
  49.9 180.2 %all-gather.3.cloned.1.call-done = f32[8192,1024]{1,0:T(8,128)} async-done(((f32[256,1024]{1,0:T(8,128)}), f32[8192,1024]{1,0:T(8,128)}) %all-gather.3.cloned.1.call-update) | async-done | bytes 33554448 | tf_op jit(solution)/shard_map/all_gather | solution.py:21
  230.1 33.2 %fusion = f32[256,8192]{1,0:T(8,128)} fusion(f32[256,1024]{1,0:T(8,128)} %subtract_multiply_fusion, f32[8192,1024]{1,0:T(8,128)} %all-gather.3.cloned.1.call-done), kind=kOutput, calls=%fused_computation.2 | convolution fusion | flops 25769803776 | bytes 42991616 | tf_op jit(solution)/shard_map/dot_general | solution.py:8
  263.3 0.0 reduce-scatter.2.cloned.1.call-update
  263.3 0.0 copy-done.2
  263.3 0.6 dynamic-slice
  264.6 0.0 copy-done
  264.6 0.0 copy-done.1
  264.6 0.6 fusion.1
  265.2 53.7 %all-reduce = f32[1024]{0:T(1024)S(1)} all-reduce(f32[1024]{0:T(1024)S(1)} %bitcast.8), channel_id=4, replica_groups=mesh['smp'=32,'par'=8] {'smp'}, use_global_device_ids=true, to_apply=%region_3.0.clone | all-reduce | flops 1024 | bytes 8192
  318.9 0.6 dynamic-slice.1
  319.5 62.4 %reduce-scatter.2.cloned.1.call-done = f32[256,1024]{1,0:T(8,128)} async-done(((f32[256,8192]{1,0:T(8,128)}), f32[256,1024]{1,0:T(8,128)}) %reduce-scatter.2.cloned.1.call-update) | async-done | bytes 1048592 | tf_op jit(solution)/shard_map/reduce_scatter | solution.py:22
  (3 shorter events, 0.1 us)
Async XLA Ops:
  7.2 257.4 %copy-start = (f32[256]{0:T(256)S(1)}, f32[256]{0:T(256)}, u32[]{:S(2)}) copy-start(f32[256]{0:T(256)} %param.3) | copy-start | bytes 3076
  7.2 222.9 %all-gather.3.cloned.1.call-start = ((), (), s32[]{:S(2)}) async-start(), calls=%async_computation.1 | async-start | bytes 34603008 | tf_op jit(solution)/shard_map/all_gather | solution.py:21
  49.8 213.5 %copy-start.2 = (u32[256]{0:T(256)S(1)}, u32[256]{0:T(256)}, u32[]{:S(2)}) copy-start(u32[256]{0:T(256)} %constant.10) | copy-start | bytes 3076
  49.8 214.7 %copy-start.1 = (f32[256,1024]{1,0:T(8,128)S(1)}, f32[256,1024]{1,0:T(8,128)}, u32[]{:S(2)}) copy-start(f32[256,1024]{1,0:T(8,128)} %subtract_multiply_fusion) | copy-start | bytes 3145732
  49.8 332.1 %reduce-scatter.2.cloned.1.call-start = ((), (), s32[]{:S(2)}) async-start(), calls=%async_computation.2 | async-start | bytes 9437184 | tf_op jit(solution)/shard_map/reduce_scatter | solution.py:22
Sparse Core Ops, SparseCore 0:
  49.9 180.0 all-gather.2
  263.4 118.4 reduce-scatter.1

commit v2 on v0

--- a/solution.py
+++ b/solution.py
@@ -18,7 +18,12 @@
     samples = log_derivs.shape[0] * lax.axis_size("smp")
     column_total = lax.psum(jnp.sum(log_derivs, axis=0), "smp")
     centred = (log_derivs - column_total[None, :] / samples) / jnp.sqrt(jnp.float32(samples))
-    partial_gram = row_products(centred, lax.all_gather(centred, "smp", axis=0, tiled=True))
+    partial_gram = row_products(
+        centred,
+        jnp.concatenate(
+            lax.all_to_all(jnp.stack([centred] * lax.axis_size("smp")), "smp", 0, 0), axis=0
+        ),
+    )
     gram = lax.psum_scatter(partial_gram, "par", scatter_dimension=1, tiled=True)
     update_term = lax.dot_general(
         coefficients,

time: 411 us -> 960 us (2.34)
  blocking collectives: 111 us -> 843 us
  waiting for transfers between devices: 246 us -> 60.1 us
    all_to_all x0 -> x1, blocking collectives: none -> 731 us  [local(): lax.all_to_all(jnp.stack([centred] * lax.axis_size('smp')), 'smp', 0, 0)]
    all_gather x1 -> x0, waiting for transfers between devices: 184 us -> none  [local(): lax.all_gather(centred, 'smp', axis=0, tiled=True)]
  transfers between devices with their start and end apart: 2 -> 1, of which waited for: 2 -> 1; matrix products, arithmetic and copies ran while one was open for 0% -> 0% of each run, Pallas kernels for 0% -> 0%
where the time goes in v2:
time: 960 us
  blocking collectives  843 us (88%)
  waiting for transfers between devices  60.1 us (6%)
  matrix products  33.6 us (4%)
  between operations  14.7 us (2%)
    all_to_all x1, blocking collectives, local(): lax.all_to_all(jnp.stack([centred] * lax.axis_size('smp')), 'smp', 0, 0)  731 us
    reduce_scatter x1, waiting for transfers between devices, local(): lax.psum_scatter(partial_gram, 'par', scatter_dimension=1, tiled=True)  60.1 us
    psum x1, blocking collectives, local(): column_total = lax.psum(jnp.sum(log_derivs, axis=0), 'smp')  56.9 us
    unnamed x1, blocking collectives  55.6 us
    dot_general x1, matrix products, row_products(): lax.dot_general(left_rows, right_rows, (((1,), (1,)), ((), ())), precisio...  33 us
  transfers between devices with their start and end apart: 1, of which 1 were waited for; matrix products, arithmetic and copies ran while one was open for 0% of the time, Pallas kernels for 0%

profile of v2, /device:TPU:1, one launch (start us, length us, event | category | flops | bytes accessed | tf_op | source)
XLA Modules:
  0.0 959.6 jit_solution(8777809159813791825)
XLA Ops:
  7.2 0.0 copy-start
  7.2 0.0 reduce-scatter.2.cloned.1.call-start
  7.2 1.3 reduce_sum.9
  8.5 56.9 %psum.7 = f32[1024]{0:T(1024)S(1)} all-reduce(f32[1024]{0:T(1024)S(1)} %reduce_sum.9), channel_id=1, replica_groups=mesh['smp'=32,'par'=8] {'smp'}, use_global_device_ids=true, to_apply=%region_1.0 | all-reduce | flops 1024 | bytes 8192 | tf_op jit(solution)/shard_map/psum | solution.py:19
  65.4 1.3 subtract_multiply_fusion
  66.8 4.3 stack.2
  71.0 730.6 %all_to_all.5 = f32[32,256,1024]{2,1,0:T(8,128)} all-to-all(f32[32,256,1024]{2,1,0:T(8,128)S(1)} %stack.2), channel_id=1, replica_groups=mesh['smp'=32,'par'=8] {'smp'}, dimensions={0} | all-to-all | bytes 67108864 | tf_op jit(solution)/shard_map/all_to_all | solution.py:24
  801.6 0.0 copy-start.1
  801.7 33.0 %fusion = f32[256,8192]{1,0:T(8,128)} fusion(f32[256,1024]{1,0:T(8,128)S(1)} %subtract_multiply_fusion, f32[8192,1024]{1,0:T(8,128)} %bitcast.9), kind=kOutput, calls=%fused_computation.2 | convolution fusion | flops 25769803776 | bytes 42991616 | tf_op jit(solution)/shard_map/dot_general | solution.py:8
  834.6 0.0 reduce-scatter.2.cloned.1.call-update
  834.7 0.0 copy-done.1
  834.7 0.6 dynamic-slice
  835.9 0.0 copy-done
  835.9 0.6 fusion.1
  836.6 55.6 %all-reduce = f32[1024]{0:T(1024)S(1)} all-reduce(f32[1024]{0:T(1024)S(1)} %bitcast.10), channel_id=3, replica_groups=mesh['smp'=32,'par'=8] {'smp'}, use_global_device_ids=true, to_apply=%region_3.0.clone | all-reduce | flops 1024 | bytes 8192
  892.1 0.6 dynamic-slice.1
  892.7 60.1 %reduce-scatter.2.cloned.1.call-done = f32[256,1024]{1,0:T(8,128)} async-done(((f32[256,8192]{1,0:T(8,128)}), f32[256,1024]{1,0:T(8,128)}) %reduce-scatter.2.cloned.1.call-update) | async-done | bytes 1048592 | tf_op jit(solution)/shard_map/reduce_scatter | solution.py:27
  (1 shorter events, 0.0 us)
Async XLA Ops:
  7.2 828.8 %copy-start = (f32[256]{0:T(256)S(1)}, f32[256]{0:T(256)}, u32[]{:S(2)}) copy-start(f32[256]{0:T(256)} %param.3) | copy-start | bytes 3076
  7.2 945.6 %reduce-scatter.2.cloned.1.call-start = ((), (), s32[]{:S(2)}) async-start(), calls=%async_computation.2 | async-start | bytes 9437184 | tf_op jit(solution)/shard_map/reduce_scatter | solution.py:27
  801.6 33.0 %copy-start.1 = (u32[256]{0:T(256)S(1)}, u32[256]{0:T(256)}, u32[]{:S(2)}) copy-start(u32[256]{0:T(256)} %constant.10) | copy-start | bytes 3076
Sparse Core Ops, SparseCore 0:
  834.8 117.9 reduce-scatter.1
